TPU v7x, 32 devices: a whole 2x2x4 slice. The times are simulated.
32 devices in a mesh: tok: 8 (over y, x, core), mdl: 4 (over z).
Axes of the slice: x: 2, y: 2, z: 4, core: 2. Of those that a mesh axis runs over, the one named last changes fastest.
Arguments:
- hidden_states: bfloat16 [4096, 3072], P('tok', 'mdl'), may hold values from -36 to 36
- lengths: int32 [2], replicated, may hold values from 1 to 2277, 3644 in all
- positions: int32 [3, 4096], P(None, 'tok'), may hold values from 0 to 44, as said below
- modulation: float32 [6, 3072], replicated, may hold values from -3 to 3
- query_weight: bfloat16 [3072, 3072], P('tok', 'mdl'), may hold values from -1.1 to 1.1
- key_weight: bfloat16 [3072, 3072], P('tok', 'mdl'), may hold values from -1.1 to 1.1
- value_weight: bfloat16 [3072, 3072], P('tok', 'mdl'), may hold values from -0.109375 to 0.109375
- out_weight: bfloat16 [3072, 3072], P('tok', 'mdl'), may hold values from -0.109375 to 0.109375
- query_gain: float32 [64], replicated, may hold values from 0.1 to 1.9
- key_gain: float32 [64], replicated, may hold values from 0.1 to 1.9
Outputs:
- updated: bfloat16 [4096, 3072], P('tok', 'mdl')
Inputs may be any that keep to these rules, and one draw needn't show every extreme that they name: lengths[0] + lengths[1] = 3644, and neither of them exceeds 2277. `positions`: frame below 13, row below 30, column below 45.
All inputs are finite; a program needn't handle non-finite values.
Results may differ from a plain program's by a relative error of at most 0.0045.
Values may be sent and summed in bfloat16 or wider, within the bound.
A program may use at most 128 MiB of HBM per device.

v0:
```python
import jax
import jax.numpy as jnp
from jax import lax
from jax.sharding import PartitionSpec as P

TEXT = 226


def token_labels(row_index, lengths):
    bound = TEXT + lengths[0]
    request = (row_index >= bound).astype(jnp.int32)
    place = row_index - request * bound
    return (request, place < TEXT, bound)


def modulate(rows_bf, modulation, is_text):
    values = rows_bf.astype(jnp.float32)
    center = values - jnp.mean(values, axis=1, keepdims=True)
    spread = jnp.mean(center * center, axis=1, keepdims=True)
    normal = center * lax.rsqrt(spread + 1e-05)
    textual = is_text[:, None]
    shift = jnp.where(textual, modulation[3][None, :], modulation[0][None, :])
    scale = jnp.where(textual, modulation[4][None, :], modulation[1][None, :])
    return (normal * (1.0 + scale) + shift).astype(jnp.bfloat16)


def pair_angles(positions, pairs):
    index = jnp.arange(pairs, dtype=jnp.int32)
    first = pairs // 4
    second = (pairs - first) // 2
    third = pairs - first - second
    component = jnp.where(index < first, 0, jnp.where(index < first + second, 1, 2))
    local = index - jnp.where(component == 0, 0, jnp.where(component == 1, first, first + second))
    count = jnp.where(component == 0, first, jnp.where(component == 1, second, third))
    rates = jnp.power(jnp.float32(10000.0), -local.astype(jnp.float32) / count.astype(jnp.float32))
    places = positions.astype(jnp.float32)
    chosen = jnp.where(
        component[:, None] == 0,
        places[0][None, :],
        jnp.where(component[:, None] == 1, places[1][None, :], places[2][None, :]),
    )
    return jnp.transpose(chosen * rates[:, None])


def head_norm(projected, gain, angles, is_text):
    width = gain.shape[0]
    shaped = projected.reshape(projected.shape[0], -1, width)
    center = shaped - jnp.mean(shaped, axis=2, keepdims=True)
    spread = jnp.mean(center * center, axis=2, keepdims=True)
    normal = center * lax.rsqrt(spread + 1e-06) * gain
    half = width // 2
    cosine = jnp.cos(angles)[:, None, :]
    sine = jnp.sin(angles)[:, None, :]
    lower = normal[:, :, :half]
    upper = normal[:, :, half:]
    turned = jnp.concatenate([lower * cosine - upper * sine, lower * sine + upper * cosine], axis=2)
    return jnp.where(is_text[:, None, None], normal, turned).astype(jnp.bfloat16)


def shards(
    hidden_states,
    lengths,
    positions,
    modulation,
    query_weight,
    key_weight,
    value_weight,
    out_weight,
    query_gain,
    key_gain,
):
    own_rows = hidden_states.shape[0]
    local_width = query_weight.shape[1]
    head_width = query_gain.shape[0]
    local_heads = local_width // head_width
    full_rows = lax.all_gather(hidden_states, "mdl", axis=1, tiled=True)
    row_index = lax.axis_index("tok") * own_rows + jnp.arange(own_rows, dtype=jnp.int32)
    request, is_text, bound = token_labels(row_index, lengths)
    normed = modulate(full_rows, modulation, is_text)
    angles = pair_angles(positions, head_width // 2)
    pieces = (
        lax.all_gather(query_weight, "tok", axis=0, tiled=True),
        lax.all_gather(key_weight, "tok", axis=0, tiled=True),
        lax.all_gather(value_weight, "tok", axis=0, tiled=True),
    )
    columns = normed
    query_sum, key_sum, value_sum = tuple(
        (
            jnp.dot(columns, pieces[number], preferred_element_type=jnp.float32)
            for number in range(3)
        )
    )
    query = head_norm(query_sum, query_gain, angles, is_text)
    key_flat = head_norm(key_sum, key_gain, angles, is_text).reshape(own_rows, local_width)
    value_flat = value_sum.astype(jnp.bfloat16)
    factor = head_width ** (-0.5)

    def block_terms(block_keys, block_values, block_start):
        size = block_keys.shape[0]
        key_request = (block_start + jnp.arange(size, dtype=jnp.int32) >= bound).astype(jnp.int32)
        score = (
            jnp.einsum(
                "qhd,khd->hqk",
                query,
                block_keys.reshape(size, local_heads, head_width),
                preferred_element_type=jnp.float32,
            )
            * factor
        )
        same = (request[:, None] == key_request[None, :])[None, :, :]
        expo = jnp.where(same, jnp.exp(score), jnp.float32(0.0))
        totals = jnp.transpose(jnp.sum(expo, axis=2))
        weighted = jnp.einsum(
            "hqk,khd->qhd",
            expo.astype(jnp.bfloat16),
            block_values.reshape(size, local_heads, head_width),
            preferred_element_type=jnp.float32,
        )
        return (weighted.reshape(own_rows, local_width), totals)

    initial = (
        jnp.zeros((own_rows, local_width), jnp.float32),
        jnp.zeros((own_rows, local_heads), jnp.float32),
    )
    keys_piece = lax.all_gather(key_flat, "tok", axis=0, tiled=True)
    values_piece = lax.all_gather(value_flat, "tok", axis=0, tiled=True)
    count = keys_piece.shape[0]
    block = 1024
    steps_count = count // block

    def step_block(inner, operands):
        block_keys, block_values, offset = operands
        weighted, totals = block_terms(block_keys, block_values, offset)
        return ((inner[0] + weighted, inner[1] + totals), None)

    offsets = jnp.arange(steps_count, dtype=jnp.int32) * block
    result, unused = lax.scan(
        step_block,
        initial,
        (
            keys_piece.reshape(steps_count, block, local_width),
            values_piece.reshape(steps_count, block, local_width),
            offsets,
        ),
    )
    weighted, totals = result
    attended = (
        (weighted.reshape(own_rows, local_heads, head_width) / totals[:, :, None])
        .reshape(own_rows, local_width)
        .astype(jnp.bfloat16)
    )
    all_heads = lax.all_gather(attended, "mdl", axis=1, tiled=True)
    out_width = out_weight.shape[1]
    columns = all_heads
    projected = jnp.dot(
        columns,
        lax.all_gather(out_weight, "tok", axis=0, tiled=True),
        preferred_element_type=jnp.float32,
    )
    gate_rows = lax.dynamic_slice_in_dim(
        modulation, lax.axis_index("mdl") * out_width, out_width, 1
    )
    gate = jnp.where(is_text[:, None], gate_rows[5][None, :], gate_rows[2][None, :])
    return (hidden_states.astype(jnp.float32) + gate * projected).astype(jnp.bfloat16)


def solution(mesh):
    return jax.shard_map(
        shards,
        mesh=mesh,
        in_specs=(
            P("tok", "mdl"),
            P(),
            P(None, "tok"),
            P(),
            P("tok", "mdl"),
            P("tok", "mdl"),
            P("tok", "mdl"),
            P("tok", "mdl"),
            P(),
            P(),
        ),
        out_specs=P("tok", "mdl"),
        check_vma=False,
    )
```

profile of v0, /device:TPU:0, one launch (start us, length us, event | category | flops | bytes accessed | tf_op | source)
XLA Modules:
  0.0 505.0 jit_solution(1737966056882740450)
XLA Ops:
  6.6 0.7 all-gather.9.cloned.1.call-update
  7.3 0.7 all-gather.15.cloned.1.call-update
  8.1 0.7 all-gather.19.cloned.1.call-update
  9.6 1.0 fusion.20
  10.6 64.5 %all-gather.9.cloned.1.call-done = bf16[512,3072]{1,0:T(8,128)(2,1)} async-done(((bf16[512,768]{1,0:T(8,128)(2,1)}), bf16[512,3072]{1,0:T(8,128)(2,1)}) %all-gather.9.cloned.1.call-update) | async-done | bytes 3145744 | tf_op jit(solution)/shard_map/all_gather | solution.py:76
  75.1 2.5 convert_reduce_fusion
  78.0 1.0 fusion.13
  78.9 3.7 fusion.16
  82.7 32.0 %all-gather.15.cloned.1.call-done = bf16[3072,768]{1,0:T(8,128)(2,1)} async-done(((bf16[384,768]{1,0:T(8,128)(2,1)}), bf16[3072,768]{1,0:T(8,128)(2,1)}) %all-gather.15.cloned.1.call-update) | async-done | bytes 4718608 | tf_op jit(solution)/shard_map/all_gather | solution.py:83
  114.7 5.9 %fusion.25 = f32[512,768]{1,0:T(8,128)S(1)} fusion(bf16[512,3072]{1,0:T(8,128)(2,1)} %fusion.16, bf16[3072,768]{1,0:T(8,128)(2,1)} %all-gather.15.cloned.1.call-done), kind=kOutput, calls=%fused_computation.64 | convolution fusion | flops 2415919104 | bytes 9437184 | tf_op jit(solution)/shard_map/dot_general | solution.py:89
  121.0 0.7 copy-done.3
  121.9 33.6 %all-gather.19.cloned.1.call-done = bf16[3072,768]{1,0:T(8,128)(2,1)} async-done(((bf16[384,768]{1,0:T(8,128)(2,1)}), bf16[3072,768]{1,0:T(8,128)(2,1)}) %all-gather.19.cloned.1.call-update) | async-done | bytes 4718608 | tf_op jit(solution)/shard_map/all_gather | solution.py:82
  155.5 5.5 %fusion.26 = f32[512,768]{0,1:T(8,128)S(1)} fusion(bf16[512,3072]{1,0:T(8,128)(2,1)} %fusion.16, bf16[3072,768]{1,0:T(8,128)(2,1)} %all-gather.19.cloned.1.call-done), kind=kOutput, calls=%fused_computation.65 | convolution fusion | flops 2415919104 | bytes 9437184 | tf_op jit(solution)/shard_map/dot_general | solution.py:89
  163.4 1.3 multiply_subtract_fusion
  164.8 1.2 copy.23
  165.9 0.9 mul.163
  166.9 1.7 copy.22
  168.5 0.9 sub.56
  169.5 1.6 copy.21
  171.1 3.8 select_convert_fusion
  175.1 21.0 %all-gather.11.cloned.1.call-done = bf16[3072,768]{1,0:T(8,128)(2,1)} async-done(((bf16[384,768]{1,0:T(8,128)(2,1)}), bf16[3072,768]{1,0:T(8,128)(2,1)}) %all-gather.11.cloned.1.call-update) | async-done | bytes 4718608 | tf_op jit(solution)/shard_map/all_gather | solution.py:84
  196.2 6.8 %convolution_convert_fusion = bf16[512,768]{1,0:T(8,128)(2,1)} fusion(bf16[512,3072]{1,0:T(8,128)(2,1)} %fusion.16, bf16[3072,768]{1,0:T(8,128)(2,1)} %all-gather.11.cloned.1.call-done), kind=kOutput, calls=%fused_computation.36 | convolution fusion | flops 2416312320 | bytes 8650752 | tf_op jit(solution)/shard_map/dot_general | solution.py:89
  203.0 0.7 all-gather.23.cloned.1.call-update
  204.0 1.3 fusion.17
  205.3 38.2 %all-gather.17.cloned.1.call-done = bf16[4096,768]{1,0:T(8,128)(2,1)} async-done(((bf16[512,768]{1,0:T(8,128)(2,1)}), bf16[4096,768]{1,0:T(8,128)(2,1)}) %all-gather.17.cloned.1.call-update) | async-done | bytes 6291472 | tf_op jit(solution)/shard_map/all_gather | solution.py:125
  243.5 47.3 %all-gather.13.cloned.1.call-done = bf16[4096,768]{1,0:T(8,128)(2,1)} async-done(((bf16[512,768]{1,0:T(8,128)(2,1)}), bf16[4096,768]{1,0:T(8,128)(2,1)}) %all-gather.13.cloned.1.call-update) | async-done | bytes 6291472 | tf_op jit(solution)/shard_map/all_gather | solution.py:126
  290.8 134.3 %while.15 = (s32[]{:T(128)}, f32[512,768]{0,1:T(8,128)}, f32[512,12]{0,1:T(8,128)}, bf16[4,1024,768]{2,1,0:T(8,128)(2,1)}, s32[4]{0:T(128)S(1)}, /*index=5*/s32[...) while((s32[]{:T(128)}, f32[512,768]{0,1:T(8,128)}, ...), condition=%wide.region_8.9_spmd.clone.clone.clone, body=%wide.region_6.8_spmd.clone.clone.clone.sunk | while | flops 1649682944 | bytes 87601416 | solution.py:137
  290.8 0.6 dynamic_slice.29
  291.4 0.6 fusion.51
  292.0 1.2 broadcast_compare_fusion.4
  293.2 2.1 constant_dynamic-slice_fusion.3
  295.3 1.6 copy.34
  296.9 13.0 %fusion.52 = (f32[12,512]{1,0:T(8,128)S(1)}, f32[12,1024,512]{2,1,0:T(8,128)}) fusion(pred[512,1024]{0,1:T(8,128)(4,1)} %broadcast_compare_fusion.4, bf16[1024,12,64]{0,2,1:T(8,128)(2,1)} %bitcast.67, bf16[512,12,64]{0,2,1:T(8,128)(2,1)} %get-tuple-element.289), kind=kOutput, calls=%fused_computation.2.clone.1 | convolution fusion | flops 824174592 | bytes 28073984 | tf_op jit(solution)/shard_map/while/body/eval_jaxpr/qhd,khd->hqk/dot_general | solution.py:102
  309.9 1.6 copy.33
  311.5 11.7 %fusion.53 = f32[12,64,512]{2,1,0:T(8,128)S(1)} fusion(bf16[1024,12,64]{0,2,1:T(8,128)(2,1)} %bitcast.68, f32[12,1024,512]{2,1,0:T(8,128)} %get-tuple-element.258, pred[512,1024]{0,1:T(8,128)(4,1)} %broadcast_compare_fusion.4), kind=kOutput, calls=%fused_computation.4.clone.1 | convolution fusion | flops 824180736 | bytes 28835840 | tf_op jit(solution)/shard_map/while/body/eval_jaxpr/hqk,khd->qhd/dot_general | solution.py:113
  324.0 0.9 copy-done.1
  325.5 0.6 fusion.51
  326.2 1.2 broadcast_compare_fusion.4
  327.3 2.1 constant_dynamic-slice_fusion.3
  329.5 1.6 copy.34
  331.1 13.0 %fusion.52 = (f32[12,512]{1,0:T(8,128)S(1)}, f32[12,1024,512]{2,1,0:T(8,128)}) fusion(pred[512,1024]{0,1:T(8,128)(4,1)} %broadcast_compare_fusion.4, bf16[1024,12,64]{0,2,1:T(8,128)(2,1)} %bitcast.67, bf16[512,12,64]{0,2,1:T(8,128)(2,1)} %get-tuple-element.289), kind=kOutput, calls=%fused_computation.2.clone.1 | convolution fusion | flops 824174592 | bytes 28073984 | tf_op jit(solution)/shard_map/while/body/eval_jaxpr/qhd,khd->hqk/dot_general | solution.py:102
  344.1 1.6 copy.33
  345.7 10.9 %fusion.53 = f32[12,64,512]{2,1,0:T(8,128)S(1)} fusion(bf16[1024,12,64]{0,2,1:T(8,128)(2,1)} %bitcast.68, f32[12,1024,512]{2,1,0:T(8,128)} %get-tuple-element.258, pred[512,1024]{0,1:T(8,128)(4,1)} %broadcast_compare_fusion.4), kind=kOutput, calls=%fused_computation.4.clone.1 | convolution fusion | flops 824180736 | bytes 28835840 | tf_op jit(solution)/shard_map/while/body/eval_jaxpr/hqk,khd->qhd/dot_general | solution.py:113
  357.4 0.9 copy-done.1
  358.9 0.6 fusion.51
  359.6 1.2 broadcast_compare_fusion.4
  360.8 2.1 constant_dynamic-slice_fusion.3
  362.8 1.6 copy.34
  364.5 13.0 %fusion.52 = (f32[12,512]{1,0:T(8,128)S(1)}, f32[12,1024,512]{2,1,0:T(8,128)}) fusion(pred[512,1024]{0,1:T(8,128)(4,1)} %broadcast_compare_fusion.4, bf16[1024,12,64]{0,2,1:T(8,128)(2,1)} %bitcast.67, bf16[512,12,64]{0,2,1:T(8,128)(2,1)} %get-tuple-element.289), kind=kOutput, calls=%fused_computation.2.clone.1 | convolution fusion | flops 824174592 | bytes 28073984 | tf_op jit(solution)/shard_map/while/body/eval_jaxpr/qhd,khd->hqk/dot_general | solution.py:102
  377.4 1.6 copy.33
  379.1 10.9 %fusion.53 = f32[12,64,512]{2,1,0:T(8,128)S(1)} fusion(bf16[1024,12,64]{0,2,1:T(8,128)(2,1)} %bitcast.68, f32[12,1024,512]{2,1,0:T(8,128)} %get-tuple-element.258, pred[512,1024]{0,1:T(8,128)(4,1)} %broadcast_compare_fusion.4), kind=kOutput, calls=%fused_computation.4.clone.1 | convolution fusion | flops 824180736 | bytes 28835840 | tf_op jit(solution)/shard_map/while/body/eval_jaxpr/hqk,khd->qhd/dot_general | solution.py:113
  390.8 0.9 copy-done.1
  392.3 0.6 fusion.51
  392.9 1.2 broadcast_compare_fusion.4
  394.1 2.1 constant_dynamic-slice_fusion.3
  396.2 1.6 copy.34
  397.8 13.0 %fusion.52 = (f32[12,512]{1,0:T(8,128)S(1)}, f32[12,1024,512]{2,1,0:T(8,128)}) fusion(pred[512,1024]{0,1:T(8,128)(4,1)} %broadcast_compare_fusion.4, bf16[1024,12,64]{0,2,1:T(8,128)(2,1)} %bitcast.67, bf16[512,12,64]{0,2,1:T(8,128)(2,1)} %get-tuple-element.289), kind=kOutput, calls=%fused_computation.2.clone.1 | convolution fusion | flops 824174592 | bytes 28073984 | tf_op jit(solution)/shard_map/while/body/eval_jaxpr/qhd,khd->hqk/dot_general | solution.py:102
  410.8 1.6 copy.33
  412.4 10.9 %fusion.53 = f32[12,64,512]{2,1,0:T(8,128)S(1)} fusion(bf16[1024,12,64]{0,2,1:T(8,128)(2,1)} %bitcast.68, f32[12,1024,512]{2,1,0:T(8,128)} %get-tuple-element.258, pred[512,1024]{0,1:T(8,128)(4,1)} %broadcast_compare_fusion.4), kind=kOutput, calls=%fused_computation.4.clone.1 | convolution fusion | flops 824180736 | bytes 28835840 | tf_op jit(solution)/shard_map/while/body/eval_jaxpr/hqk,khd->qhd/dot_general | solution.py:113
  424.1 0.9 copy-done.1
  425.0 2.5 fusion.18
  427.6 0.9 dynamic-slice_reduce_fusion.1
  428.6 62.7 %all-gather.21.cloned.1.call-done = bf16[512,3072]{0,1:T(8,128)(2,1)} async-done(((bf16[512,768]{0,1:T(8,128)(2,1)}), bf16[512,3072]{0,1:T(8,128)(2,1)}) %all-gather.21.cloned.1.call-update) | async-done | bytes 3145744 | tf_op jit(solution)/shard_map/all_gather | solution.py:152
  491.3 6.9 %add_convert_fusion = bf16[512,768]{1,0:T(8,128)(2,1)} fusion(bf16[512,768]{1,0:T(8,128)(2,1)S(1)} %copy-done.7, bf16[512,3072]{0,1:T(8,128)(2,1)} %all-gather.21.cloned.1.call-done, bf16[3072,768]{1,0:T(8,128)(2,1)} %all-gather.23.cloned.1.call-done, f32[768]{0:T(1024)S(1)} %get-tuple-element.157, f32[768]{0:T(1024)S(1)} %get-tuple-element.156, ...), kind=kOutput, calls=%fused_computation.30 | convolution fusion | flops 2417885184 | bytes 9443840 | tf_op jit(solution)/shard_map/dot_general | solution.py:155
  (118 shorter events, 9.6 us)
Async XLA Ops:
  6.5 2.9 copy-start.17
  6.5 2.9 copy-start.21
  6.5 3.0 copy-start.22
  6.5 4.1 copy-start.16
  6.5 68.6 %all-gather.9.cloned.1.call-start = ((), (), s32[]{:S(2)}) async-start(), calls=%async_computation | async-start | bytes 3932160 | tf_op jit(solution)/shard_map/all_gather | solution.py:76
  7.3 107.4 %all-gather.15.cloned.1.call-start = ((), (), s32[]{:S(2)}) async-start(), calls=%async_computation.3 | async-start | bytes 5308416 | tf_op jit(solution)/shard_map/all_gather | solution.py:83
  8.0 147.5 %all-gather.19.cloned.1.call-start = ((), (), s32[]{:S(2)}) async-start(), calls=%async_computation.5 | async-start | bytes 5308416 | tf_op jit(solution)/shard_map/all_gather | solution.py:82
  8.8 187.4 %all-gather.11.cloned.1.call-start = ((), (), s32[]{:S(2)}) async-start(), calls=%async_computation.1 | async-start | bytes 5308416 | tf_op jit(solution)/shard_map/all_gather | solution.py:84
  9.3 234.1 %all-gather.17.cloned.1.call-start = ((), (), s32[]{:S(2)}) async-start(), calls=%async_computation.4 | async-start | bytes 7077888 | tf_op jit(solution)/shard_map/all_gather | solution.py:125
  9.6 194.2 %copy-start.18 = (pred[512]{0:T(512)(128)(4,1)}, pred[512]{0:T(512)(128)(4,1)S(1)}, u32[]{:S(2)}) copy-start(pred[512]{0:T(512)(128)(4,1)S(1)} %subtract_compare_fusion) | copy-start | bytes 1540
  75.1 2.8 copy-start.2
  120.6 1.1 copy-start.3
  161.2 0.6 copy-start.10
  161.5 0.7 copy-start.8
  161.8 0.6 copy-start.13
  161.8 0.6 copy-start.11
  161.9 0.7 copy-start.20
  162.5 0.8 copy-start.14
  162.5 0.9 copy-start.15
  174.9 28.9 %copy-start.9 = (f32[512,12]{0,1:T(8,128)S(1)}, f32[512,12]{0,1:T(8,128)}, u32[]{:S(2)}) copy-start(f32[512,12]{0,1:T(8,128)} %copy-done.8) | copy-start | bytes 73732
  174.9 28.9 %copy-start.12 = (f32[512,12]{0,1:T(8,128)S(1)}, f32[512,12]{0,1:T(8,128)}, u32[]{:S(2)}) copy-start(f32[512,12]{0,1:T(8,128)} %copy-done.11) | copy-start | bytes 73732
  174.9 115.9 %all-gather.13.cloned.1.call-start = ((), (), s32[]{:S(2)}) async-start(), calls=%async_computation.2 | async-start | bytes 7077888 | tf_op jit(solution)/shard_map/all_gather | solution.py:126
  203.0 1.0 copy-start.4
  203.0 225.6 %all-gather.23.cloned.1.call-start = ((), (), s32[]{:S(2)}) async-start(), calls=%async_computation.7 | async-start | bytes 5308416 | tf_op jit(solution)/shard_map/all_gather | solution.py:157
  203.7 287.5 %all-gather.21.cloned.1.call-start = ((), (), s32[]{:S(2)}) async-start(), calls=%async_computation.6 | async-start | bytes 3932160 | tf_op jit(solution)/shard_map/all_gather | solution.py:152
  311.5 11.7 %copy-start = (f32[512,768]{0,1:T(8,128)S(1)}, f32[512,768]{0,1:T(8,128)}, u32[]{:S(2)}) copy-start(f32[512,768]{0,1:T(8,128)} %get-tuple-element.272) | copy-start | bytes 4718596 | tf_op jit(solution)/shard_map/while
  323.2 0.8 copy-start.5
  323.7 1.2 copy-start.1
  324.0 0.9 copy-start.6
  345.7 10.9 %copy-start = (f32[512,768]{0,1:T(8,128)S(1)}, f32[512,768]{0,1:T(8,128)}, u32[]{:S(2)}) copy-start(f32[512,768]{0,1:T(8,128)} %get-tuple-element.272) | copy-start | bytes 4718596 | tf_op jit(solution)/shard_map/while
  356.6 0.8 copy-start.5
  357.1 1.2 copy-start.1
  357.4 0.9 copy-start.6
  379.1 10.9 %copy-start = (f32[512,768]{0,1:T(8,128)S(1)}, f32[512,768]{0,1:T(8,128)}, u32[]{:S(2)}) copy-start(f32[512,768]{0,1:T(8,128)} %get-tuple-element.272) | copy-start | bytes 4718596 | tf_op jit(solution)/shard_map/while
  390.0 0.8 copy-start.5
  390.5 1.2 copy-start.1
  390.8 0.9 copy-start.6
  412.4 10.9 %copy-start = (f32[512,768]{0,1:T(8,128)S(1)}, f32[512,768]{0,1:T(8,128)}, u32[]{:S(2)}) copy-start(f32[512,768]{0,1:T(8,128)} %get-tuple-element.272) | copy-start | bytes 4718596 | tf_op jit(solution)/shard_map/while
  423.3 0.8 copy-start.5
  423.8 1.2 copy-start.1
  424.1 0.9 copy-start.6
  425.0 66.2 %copy-start.7 = (bf16[512,768]{1,0:T(8,128)(2,1)S(1)}, bf16[512,768]{1,0:T(8,128)(2,1)}, u32[]{:S(2)}) copy-start(bf16[512,768]{1,0:T(8,128)(2,1)} %param.12) | copy-start | bytes 2359300
  425.0 66.2 %copy-start.19 = (pred[512]{0:T(512)(128)(4,1)S(1)}, pred[512]{0:T(512)(128)(4,1)}, u32[]{:S(2)}) copy-start(pred[512]{0:T(512)(128)(4,1)} %copy-done.18) | copy-start | bytes 1540
Sparse Core Ops, SparseCore 0:
  8.9 66.1 all-gather.8
  77.0 37.5 all-gather.14
  116.5 38.9 all-gather.18
  157.2 38.9 all-gather.10
  197.9 45.5 all-gather.16
  245.2 45.5 all-gather.12
  292.7 38.9 all-gather.22
  427.7 63.4 all-gather.20
where the time goes:
time: 506 us; the launch traced here: 505 us
  waiting for transfers between devices  303 us (60%)
  matrix products  121 us (24%)
  local copies, waits for them, and re-layouts  38.3 us (8%)
  other arithmetic  28 us (6%)
  between operations  13.9 us (3%)
    all_gather x1, waiting for transfers between devices, shards(): full_rows = lax.all_gather(hidden_states, 'mdl', axis=1, tiled=True)  64.5 us
    all_gather x1, waiting for transfers between devices, shards(): all_heads = lax.all_gather(attended, 'mdl', axis=1, tiled=True)  62.7 us
    dot_general x4, matrix products, block_terms(): jnp.einsum('qhd,khd->hqk', query, block_keys.reshape(size, local_heads, h...  51.9 us
    all_gather x1, waiting for transfers between devices, shards(): values_piece = lax.all_gather(value_flat, 'tok', axis=0, tiled=True)  47.3 us
    dot_general x4, matrix products, block_terms(): jnp.einsum('hqk,khd->qhd', expo.astype(jnp.bfloat16), block_values.reshap...  44.4 us
    all_gather x1, waiting for transfers between devices, shards(): keys_piece = lax.all_gather(key_flat, 'tok', axis=0, tiled=True)  38.2 us
    all_gather x1, waiting for transfers between devices, shards(): lax.all_gather(query_weight, 'tok', axis=0, tiled=True)  33.6 us
    all_gather x1, waiting for transfers between devices, shards(): lax.all_gather(key_weight, 'tok', axis=0, tiled=True)  32 us
  transfers between devices with their start and end apart: 8, of which 7 were waited for; matrix products, arithmetic and copies ran while one was open for 34% of the time, Pallas kernels for 0%

commit v1 on v0

--- a/solution.py
+++ b/solution.py
@@ -2,8 +2,16 @@
 import jax.numpy as jnp
 from jax import lax
 from jax.sharding import PartitionSpec as P
+from jax.lax import axis_index, axis_size, ppermute
 
 TEXT = 226
+
+
+def _draw_state(row_data, dim_k):
+    arr_now = list(row_data.shape[1:])
+    arr_now[dim_k] *= row_data.shape[0]
+    t_next = jnp.moveaxis(row_data, 0, dim_k).reshape(arr_now)
+    return t_next
 
 
 def token_labels(row_index, lengths):
@@ -78,8 +86,25 @@
     request, is_text, bound = token_labels(row_index, lengths)
     normed = modulate(full_rows, modulation, is_text)
     angles = pair_angles(positions, head_width // 2)
+
+    def review_the_body(payload, ax_name, at_axis):
+        world_n = axis_size(ax_name)
+        sides = [(j, (j + 1) % world_n) for j in range(world_n)]
+        block_out, field_out = ([], [])
+        xs_all = [(h, u) for u, h in sides]
+        for kk in [*range(world_n - 1)]:
+            if kk % 2 == 0:
+                block_out.append(ppermute(block_out[-1] if block_out else payload, ax_name, sides))
+            else:
+                field_out.append(ppermute(field_out[-1] if field_out else payload, ax_name, xs_all))
+        local_next = jnp.stack([*block_out[::-1], payload, *field_out], axis=0)
+        r1 = axis_index(ax_name) - len(block_out)
+        local_next = local_next[(jnp.arange(world_n) - r1) % world_n]
+        arr_next = _draw_state(local_next, at_axis)
+        return arr_next
+
     pieces = (
-        lax.all_gather(query_weight, "tok", axis=0, tiled=True),
+        review_the_body(query_weight, "tok", 0),
         lax.all_gather(key_weight, "tok", axis=0, tiled=True),
         lax.all_gather(value_weight, "tok", axis=0, tiled=True),
     )

time: 506 us -> 465 us (0.919)
  waiting for transfers between devices: 303 us -> 224 us
  local copies, waits for them, and re-layouts: 38.3 us -> 64.2 us
  starting transfers between devices: 0.49 us -> 8.86 us
    all_gather x1, waiting for transfers between devices: 64.5 us -> 0.01 us  [shards(): full_rows = lax.all_gather(hidden_states, 'mdl', axis=1, tiled=True)]
    ppermute x0 -> x7, waiting for transfers between devices: none -> 34.2 us  [the longest x4 34.2 us: review_the_body(): ppermute(block_out[-1] if block_out else payload, ax_name, sides)]
    all_gather x1 -> x0, waiting for transfers between devices: 33.6 us -> none  [shards(): lax.all_gather(query_weight, 'tok', axis=0, tiled=True)]
    all_gather x1, waiting for transfers between devices: 32 us -> 21.1 us  [shards(): lax.all_gather(key_weight, 'tok', axis=0, tiled=True)]
    ppermute x0 -> x7, starting transfers between devices: none -> 8.44 us  [the longest x3 7.93 us: review_the_body(): ppermute(field_out[-1] if field_out else payload, ax_name, xs_all)]
    dot_general x1 -> x2, local copies, waits for them, and re-layouts: 0.47 us -> 8.55 us  [shards(): jnp.dot(columns, pieces[number], preferred_element_type=jnp.float32)]
    unnamed x38 -> x53, local copies, waits for them, and re-layouts: 1.93 us -> 9.36 us
    gather x0 -> x1, local copies, waits for them, and re-layouts: none -> 5.45 us  [review_the_body(): local_next = local_next[(jnp.arange(world_n) - r1) % world_n]]
  transfers between devices with their start and end apart: 8 -> 14, of which waited for: 7 -> 9; matrix products, arithmetic and copies ran while one was open for 34% -> 44% of each run, Pallas kernels for 0% -> 0%
where the time goes in v1:
time: 465 us; the launch traced here: 464 us
  waiting for transfers between devices  224 us (48%)
  matrix products  120 us (26%)
  local copies, waits for them, and re-layouts  64.2 us (14%)
  other arithmetic  32.5 us (7%)
  between operations  14.5 us (3%)
  starting transfers between devices  8.86 us (2%)
    all_gather x1, waiting for transfers between devices, shards(): all_heads = lax.all_gather(attended, 'mdl', axis=1, tiled=True)  62.7 us
    dot_general x4, matrix products, block_terms(): jnp.einsum('qhd,khd->hqk', query, block_keys.reshape(size, local_heads, h...  51.8 us
    all_gather x1, waiting for transfers between devices, shards(): values_piece = lax.all_gather(value_flat, 'tok', axis=0, tiled=True)  47.3 us
    dot_general x4, matrix products, block_terms(): jnp.einsum('hqk,khd->qhd', expo.astype(jnp.bfloat16), block_values.reshap...  44.4 us
    all_gather x1, waiting for transfers between devices, shards(): keys_piece = lax.all_gather(key_flat, 'tok', axis=0, tiled=True)  38.5 us
    ppermute x4, waiting for transfers between devices, review_the_body(): ppermute(block_out[-1] if block_out else payload, ax_name, sides)  34.2 us
    dynamic_slice x16, local copies, waits for them, and re-layouts, shards(): lax.scan(step_block, initial, (keys_piece.reshape(steps_count, block, loc...  23.6 us
    all_gather x1, waiting for transfers between devices, shards(): lax.all_gather(key_weight, 'tok', axis=0, tiled=True)  21.1 us
  transfers between devices with their start and end apart: 14, of which 9 were waited for; matrix products, arithmetic and copies ran while one was open for 44% of the time, Pallas kernels for 0%

profile of v1, /device:TPU:0, one launch (start us, length us, event | category | flops | bytes accessed | tf_op | source)
XLA Modules:
  0.0 464.0 jit_solution(3265625731233505681)
XLA Ops:
  8.6 10.7 %collective-permute-done = bf16[384,768]{1,0:T(8,128)(2,1)S(1)} collective-permute-done((bf16[384,768]{1,0:T(8,128)(2,1)}, bf16[384,768]{1,0:T(8,128)(2,1)S(1)}, u32[]{:S(2)}, u32[]{:S(2)}) %collective-permute-start) | collective-permute-done | bytes 589856 | tf_op jit(solution)/shard_map/ppermute | solution.py:97
  19.2 2.6 collective-permute-start.4
  23.8 10.0 %collective-permute-done.1 = bf16[384,768]{1,0:T(8,128)(2,1)S(1)} collective-permute-done((bf16[384,768]{1,0:T(8,128)(2,1)S(1)}, bf16[384,768]{1,0:T(8,128)(2,1)S(1)}, u32[]{:S(2)}, u32[]{:S(2)}) %collective-permute-start.1) | collective-permute-done | bytes 589856 | tf_op jit(solution)/shard_map/ppermute | solution.py:97
  33.8 1.7 fusion.27
  35.5 2.6 collective-permute-start.5
  38.2 10.4 %collective-permute-done.2 = bf16[384,768]{1,0:T(8,128)(2,1)S(1)} collective-permute-done((bf16[384,768]{1,0:T(8,128)(2,1)S(1)}, bf16[384,768]{1,0:T(8,128)(2,1)S(1)}, u32[]{:S(2)}, u32[]{:S(2)}) %collective-permute-start.2) | collective-permute-done | bytes 589856 | tf_op jit(solution)/shard_map/ppermute | solution.py:97
  49.9 1.7 fusion.22
  52.1 1.2 mul.166
  54.1 1.3 pad_clamp_fusion
  55.4 2.6 collective-permute-start.6
  58.0 3.1 collective-permute-done.3
  61.1 1.9 bitcast_dynamic-update-slice_fusion.7
  69.1 5.5 %gather_fusion = bf16[8,384,768]{2,1,0:T(8,128)(2,1)} fusion(bf16[8,384,768]{2,1,0:T(8,128)(2,1)} %bitcast_dynamic-update-slice_fusion, s32[1024]{0:T(1024)} %pad_clamp_fusion), kind=kCustom, calls=%fused_computation | custom fusion | bytes 9437216 | tf_op jit(solution)/shard_map/gather | solution.py:102
  74.5 6.6 %copy.24 = bf16[768,3072]{1,0:T(8,128)(2,1)} copy(bf16[768,3072]{0,1:T(8,128)(2,1)} %bitcast.97) | data formatting | bytes 9437184 | tf_op jit(solution)/shard_map/dot_general | solution.py:114
  81.2 2.8 convert_reduce_fusion
  84.4 1.0 fusion.13
  85.4 2.6 fusion.16
  88.1 2.6 fusion.29
  92.0 1.6 multiply_multiply_fusion
  93.5 21.1 %all-gather.14.cloned.1.call-done = bf16[3072,768]{1,0:T(8,128)(2,1)} async-done(((bf16[384,768]{1,0:T(8,128)(2,1)}), bf16[3072,768]{1,0:T(8,128)(2,1)}) %all-gather.14.cloned.1.call-update) | async-done | bytes 4718608 | tf_op jit(solution)/shard_map/all_gather | solution.py:108
  114.6 7.0 %fusion.30 = f32[512,768]{1,0:T(8,128)} fusion(bf16[512,3072]{1,0:T(8,128)(2,1)} %copy-done.5, bf16[3072,768]{1,0:T(8,128)(2,1)} %all-gather.14.cloned.1.call-done), kind=kOutput, calls=%fused_computation.83 | convolution fusion | flops 2415919104 | bytes 9437184 | tf_op jit(solution)/shard_map/dot_general | solution.py:114
  121.7 1.9 copy.20
  125.3 1.3 multiply_subtract_fusion
  126.7 1.2 copy.23
  127.9 0.9 mul.163
  128.8 1.7 copy.22
  130.5 0.9 sub.72
  131.4 1.6 copy.21
  133.1 3.8 select_convert_fusion
  137.1 18.4 %all-gather.10.cloned.1.call-done = bf16[3072,768]{1,0:T(8,128)(2,1)} async-done(((bf16[384,768]{1,0:T(8,128)(2,1)}), bf16[3072,768]{1,0:T(8,128)(2,1)}) %all-gather.10.cloned.1.call-update) | async-done | bytes 4718608 | tf_op jit(solution)/shard_map/all_gather | solution.py:109
  155.5 6.8 %convolution_convert_fusion = bf16[512,768]{1,0:T(8,128)(2,1)} fusion(bf16[512,3072]{1,0:T(8,128)(2,1)} %copy-done.5, bf16[3072,768]{1,0:T(8,128)(2,1)} %all-gather.10.cloned.1.call-done), kind=kOutput, calls=%fused_computation.39 | convolution fusion | flops 2416312320 | bytes 8650752 | tf_op jit(solution)/shard_map/dot_general | solution.py:114
  163.0 1.3 fusion.19
  164.3 38.5 %all-gather.16.cloned.1.call-done = bf16[4096,768]{1,0:T(8,128)(2,1)} async-done(((bf16[512,768]{1,0:T(8,128)(2,1)}), bf16[4096,768]{1,0:T(8,128)(2,1)}) %all-gather.16.cloned.1.call-update) | async-done | bytes 6291472 | tf_op jit(solution)/shard_map/all_gather | solution.py:150
  202.8 47.3 %all-gather.12.cloned.1.call-done = bf16[4096,768]{1,0:T(8,128)(2,1)} async-done(((bf16[512,768]{1,0:T(8,128)(2,1)}), bf16[4096,768]{1,0:T(8,128)(2,1)}) %all-gather.12.cloned.1.call-update) | async-done | bytes 6291472 | tf_op jit(solution)/shard_map/all_gather | solution.py:151
  250.1 134.0 %while.15 = (s32[]{:T(128)}, f32[512,768]{0,1:T(8,128)}, f32[512,12]{0,1:T(8,128)}, bf16[4,1024,768]{2,1,0:T(8,128)(2,1)}, s32[4]{0:T(128)S(1)}, /*index=5*/s32[...) while((s32[]{:T(128)}, f32[512,768]{0,1:T(8,128)}, ...), condition=%wide.region_8.9_spmd.clone.clone.clone, body=%wide.region_6.8_spmd.clone.clone.clone.sunk | while | flops 1649682944 | bytes 87601416 | solution.py:162
  251.3 1.2 broadcast_compare_fusion.4
  252.5 2.1 constant_dynamic-slice_fusion.3
  254.6 1.6 copy.33
  256.2 13.0 %fusion.55 = (f32[12,512]{1,0:T(8,128)S(1)}, f32[12,1024,512]{2,1,0:T(8,128)}) fusion(pred[512,1024]{0,1:T(8,128)(4,1)} %broadcast_compare_fusion.4, bf16[1024,12,64]{0,2,1:T(8,128)(2,1)} %bitcast.92, bf16[512,12,64]{0,2,1:T(8,128)(2,1)} %get-tuple-element.291), kind=kOutput, calls=%fused_computation.3.clone.1 | convolution fusion | flops 824174592 | bytes 28073984 | tf_op jit(solution)/shard_map/while/body/eval_jaxpr/qhd,khd->hqk/dot_general | solution.py:127
  269.1 1.6 copy.32
  270.8 11.7 %fusion.56 = f32[12,64,512]{2,1,0:T(8,128)S(1)} fusion(bf16[1024,12,64]{0,2,1:T(8,128)(2,1)} %bitcast.93, f32[12,1024,512]{2,1,0:T(8,128)} %get-tuple-element.260, pred[512,1024]{0,1:T(8,128)(4,1)} %broadcast_compare_fusion.4), kind=kOutput, calls=%fused_computation.5.clone.1 | convolution fusion | flops 824180736 | bytes 28835840 | tf_op jit(solution)/shard_map/while/body/eval_jaxpr/hqk,khd->qhd/dot_general | solution.py:138
  285.4 1.2 broadcast_compare_fusion.4
  286.6 2.1 constant_dynamic-slice_fusion.3
  288.7 1.6 copy.33
  290.3 13.0 %fusion.55 = (f32[12,512]{1,0:T(8,128)S(1)}, f32[12,1024,512]{2,1,0:T(8,128)}) fusion(pred[512,1024]{0,1:T(8,128)(4,1)} %broadcast_compare_fusion.4, bf16[1024,12,64]{0,2,1:T(8,128)(2,1)} %bitcast.92, bf16[512,12,64]{0,2,1:T(8,128)(2,1)} %get-tuple-element.291), kind=kOutput, calls=%fused_computation.3.clone.1 | convolution fusion | flops 824174592 | bytes 28073984 | tf_op jit(solution)/shard_map/while/body/eval_jaxpr/qhd,khd->hqk/dot_general | solution.py:127
  303.3 1.6 copy.32
  304.9 10.9 %fusion.56 = f32[12,64,512]{2,1,0:T(8,128)S(1)} fusion(bf16[1024,12,64]{0,2,1:T(8,128)(2,1)} %bitcast.93, f32[12,1024,512]{2,1,0:T(8,128)} %get-tuple-element.260, pred[512,1024]{0,1:T(8,128)(4,1)} %broadcast_compare_fusion.4), kind=kOutput, calls=%fused_computation.5.clone.1 | convolution fusion | flops 824180736 | bytes 28835840 | tf_op jit(solution)/shard_map/while/body/eval_jaxpr/hqk,khd->qhd/dot_general | solution.py:138
  316.5 0.9 copy-done.1
  318.7 1.2 broadcast_compare_fusion.4
  319.9 2.1 constant_dynamic-slice_fusion.3
  322.0 1.6 copy.33
  323.6 13.0 %fusion.55 = (f32[12,512]{1,0:T(8,128)S(1)}, f32[12,1024,512]{2,1,0:T(8,128)}) fusion(pred[512,1024]{0,1:T(8,128)(4,1)} %broadcast_compare_fusion.4, bf16[1024,12,64]{0,2,1:T(8,128)(2,1)} %bitcast.92, bf16[512,12,64]{0,2,1:T(8,128)(2,1)} %get-tuple-element.291), kind=kOutput, calls=%fused_computation.3.clone.1 | convolution fusion | flops 824174592 | bytes 28073984 | tf_op jit(solution)/shard_map/while/body/eval_jaxpr/qhd,khd->hqk/dot_general | solution.py:127
  336.6 1.6 copy.32
  338.2 10.9 %fusion.56 = f32[12,64,512]{2,1,0:T(8,128)S(1)} fusion(bf16[1024,12,64]{0,2,1:T(8,128)(2,1)} %bitcast.93, f32[12,1024,512]{2,1,0:T(8,128)} %get-tuple-element.260, pred[512,1024]{0,1:T(8,128)(4,1)} %broadcast_compare_fusion.4), kind=kOutput, calls=%fused_computation.5.clone.1 | convolution fusion | flops 824180736 | bytes 28835840 | tf_op jit(solution)/shard_map/while/body/eval_jaxpr/hqk,khd->qhd/dot_general | solution.py:138
  349.8 0.9 copy-done.1
  352.0 1.2 broadcast_compare_fusion.4
  353.2 2.1 constant_dynamic-slice_fusion.3
  355.3 1.6 copy.33
  356.9 13.0 %fusion.55 = (f32[12,512]{1,0:T(8,128)S(1)}, f32[12,1024,512]{2,1,0:T(8,128)}) fusion(pred[512,1024]{0,1:T(8,128)(4,1)} %broadcast_compare_fusion.4, bf16[1024,12,64]{0,2,1:T(8,128)(2,1)} %bitcast.92, bf16[512,12,64]{0,2,1:T(8,128)(2,1)} %get-tuple-element.291), kind=kOutput, calls=%fused_computation.3.clone.1 | convolution fusion | flops 824174592 | bytes 28073984 | tf_op jit(solution)/shard_map/while/body/eval_jaxpr/qhd,khd->hqk/dot_general | solution.py:127
  369.9 1.6 copy.32
  371.5 10.9 %fusion.56 = f32[12,64,512]{2,1,0:T(8,128)S(1)} fusion(bf16[1024,12,64]{0,2,1:T(8,128)(2,1)} %bitcast.93, f32[12,1024,512]{2,1,0:T(8,128)} %get-tuple-element.260, pred[512,1024]{0,1:T(8,128)(4,1)} %broadcast_compare_fusion.4), kind=kOutput, calls=%fused_computation.5.clone.1 | convolution fusion | flops 824180736 | bytes 28835840 | tf_op jit(solution)/shard_map/while/body/eval_jaxpr/hqk,khd->qhd/dot_general | solution.py:138
  384.1 2.5 fusion.20
  387.6 62.7 %all-gather.18.cloned.1.call-done = bf16[512,3072]{0,1:T(8,128)(2,1)} async-done(((bf16[512,768]{0,1:T(8,128)(2,1)}), bf16[512,3072]{0,1:T(8,128)(2,1)}) %all-gather.18.cloned.1.call-update) | async-done | bytes 3145744 | tf_op jit(solution)/shard_map/all_gather | solution.py:177
  450.3 6.9 %add_convert_fusion = bf16[512,768]{1,0:T(8,128)(2,1)} fusion(bf16[512,768]{1,0:T(8,128)(2,1)S(1)} %copy-done.9, bf16[512,3072]{0,1:T(8,128)(2,1)} %all-gather.18.cloned.1.call-done, bf16[3072,768]{1,0:T(8,128)(2,1)} %all-gather.20.cloned.1.call-done, f32[768]{0:T(1024)S(1)} %get-tuple-element.157, f32[768]{0:T(1024)S(1)} %get-tuple-element.156, ...), kind=kOutput, calls=%fused_computation.33 | convolution fusion | flops 2417885184 | bytes 9443840 | tf_op jit(solution)/shard_map/dot_general | solution.py:180
  (148 shorter events, 26.8 us)
Async XLA Ops:
  6.5 74.6 %all-gather.8.cloned.1.call-start = ((), (), s32[]{:S(2)}) async-start(), calls=%async_computation | async-start | bytes 3932160 | tf_op jit(solution)/shard_map/all_gather | solution.py:84
  7.3 58.3 %copy-start.10 = (bf16[384,768]{1,0:T(8,128)(2,1)S(1)}, bf16[384,768]{1,0:T(8,128)(2,1)}, u32[]{:S(2)}) copy-start(bf16[384,768]{1,0:T(8,128)(2,1)} %param.16) | copy-start | bytes 1769476
  7.3 107.4 %all-gather.14.cloned.1.call-start = ((), (), s32[]{:S(2)}) async-start(), calls=%async_computation.3 | async-start | bytes 5308416 | tf_op jit(solution)/shard_map/all_gather | solution.py:108
  8.0 147.5 %all-gather.10.cloned.1.call-start = ((), (), s32[]{:S(2)}) async-start(), calls=%async_computation.1 | async-start | bytes 5308416 | tf_op jit(solution)/shard_map/all_gather | solution.py:109
  8.1 11.2 %collective-permute-start = (bf16[384,768]{1,0:T(8,128)(2,1)}, bf16[384,768]{1,0:T(8,128)(2,1)S(1)}, u32[]{:S(2)}, u32[]{:S(2)}) collective-permute-start(bf16[384,768]{1,0:T(8,128)(2,1)} %param.16), channel_id=1, source_target_pairs={{0,4},{4,8},{8,12},{12,16},{16,20},{20,24},{24,28},{28,0},{1,5},{5... | collective-permute-start | bytes 1769480 | tf_op jit(solution)/shard_map/ppermute | solution.py:97
  19.2 14.6 %collective-permute-start.1 = (bf16[384,768]{1,0:T(8,128)(2,1)S(1)}, bf16[384,768]{1,0:T(8,128)(2,1)S(1)}, u32[]{:S(2)}, u32[]{:S(2)}) collective-permute-start(bf16[384,768]{1,0:T(8,128)(2,1)S(1)} %collective-permute-done), channel_id=1, source_target_pairs={{0,4},{4,8},{8,12},{12,16},{16,20},{20,24},{24,28},{28,0},{1,5},{5... | collective-permute-start | bytes 1769480 | tf_op jit(solution)/shard_map/ppermute | solution.py:97
  19.2 16.3 %collective-permute-start.4 = (bf16[384,768]{1,0:T(8,128)(2,1)}, bf16[384,768]{1,0:T(8,128)(2,1)S(1)}, u32[]{:S(2)}, u32[]{:S(2)}) collective-permute-start(bf16[384,768]{1,0:T(8,128)(2,1)} %param.16), channel_id=1, source_target_pairs={{4,0},{8,4},{12,8},{16,12},{20,16},{24,20},{28,24},{0,28},{5,1},{9... | collective-permute-start | bytes 1769480 | tf_op jit(solution)/shard_map/ppermute | solution.py:99
  21.9 180.9 %all-gather.16.cloned.1.call-start = ((), (), s32[]{:S(2)}) async-start(), calls=%async_computation.4 | async-start | bytes 7077888 | tf_op jit(solution)/shard_map/all_gather | solution.py:150
  33.8 14.8 %collective-permute-start.2 = (bf16[384,768]{1,0:T(8,128)(2,1)S(1)}, bf16[384,768]{1,0:T(8,128)(2,1)S(1)}, u32[]{:S(2)}, u32[]{:S(2)}) collective-permute-start(bf16[384,768]{1,0:T(8,128)(2,1)S(1)} %collective-permute-done.1), channel_id=1, source_target_pairs={{0,4},{4,8},{8,12},{12,16},{16,20},{20,24},{24,28},{28,0},{1,5},{5... | collective-permute-start | bytes 1769480 | tf_op jit(solution)/shard_map/ppermute | solution.py:97
  35.5 19.9 %collective-permute-start.5 = (bf16[384,768]{1,0:T(8,128)(2,1)S(1)}, bf16[384,768]{1,0:T(8,128)(2,1)S(1)}, u32[]{:S(2)}, u32[]{:S(2)}) collective-permute-start(bf16[384,768]{1,0:T(8,128)(2,1)S(1)} %collective-permute-done.4), channel_id=1, source_target_pairs={{4,0},{8,4},{12,8},{16,12},{20,16},{24,20},{28,24},{0,28},{5,1},{9... | collective-permute-start | bytes 1769480 | tf_op jit(solution)/shard_map/ppermute | solution.py:99
  48.6 12.5 %collective-permute-start.3 = (bf16[384,768]{1,0:T(8,128)(2,1)S(1)}, bf16[384,768]{1,0:T(8,128)(2,1)}, u32[]{:S(2)}, u32[]{:S(2)}) collective-permute-start(bf16[384,768]{1,0:T(8,128)(2,1)S(1)} %collective-permute-done.2), channel_id=1, source_target_pairs={{0,4},{4,8},{8,12},{12,16},{16,20},{20,24},{24,28},{28,0},{1,5},{5... | collective-permute-start | bytes 1769480 | tf_op jit(solution)/shard_map/ppermute | solution.py:97
  55.4 12.8 %collective-permute-start.6 = (bf16[384,768]{1,0:T(8,128)(2,1)S(1)}, bf16[384,768]{1,0:T(8,128)(2,1)S(1)}, u32[]{:S(2)}, u32[]{:S(2)}) collective-permute-start(bf16[384,768]{1,0:T(8,128)(2,1)S(1)} %collective-permute-done.5), channel_id=1, source_target_pairs={{4,0},{8,4},{12,8},{16,12},{20,16},{24,20},{28,24},{0,28},{5,1},{9... | collective-permute-start | bytes 1769480 | tf_op jit(solution)/shard_map/ppermute | solution.py:99
  81.2 4.2 copy-start.22
  81.2 3.3 copy-start.2
  81.2 4.2 copy-start.19
  81.2 4.2 copy-start.20
  81.2 4.2 copy-start.21
  85.4 2.6 copy-start.4
  88.0 2.7 copy-start.5
  88.1 3.9 copy-start.25
  90.7 0.6 copy-start.11
  91.3 0.6 copy-start.14
  121.7 2.5 copy-start.26
  123.8 1.5 copy-start.3
  123.8 1.5 copy-start.17
  123.9 1.5 copy-start.18
  123.9 0.7 copy-start.13
  124.2 0.6 copy-start.16
  130.5 2.6 copy-start.23
  136.9 26.1 %copy-start.6 = (bf16[512,12,32]{0,2,1:T(8,128)(2,1)S(1)}, bf16[512,12,32]{0,2,1:T(8,128)(2,1)}, u32[]{:S(2)}) copy-start(bf16[512,12,32]{0,2,1:T(8,128)(2,1)} %get-tuple-element.181) | copy-start | bytes 1179652
  136.9 26.1 %copy-start.12 = (f32[512,12]{0,1:T(8,128)S(1)}, f32[512,12]{0,1:T(8,128)}, u32[]{:S(2)}) copy-start(f32[512,12]{0,1:T(8,128)} %copy-done.11) | copy-start | bytes 73732
  136.9 26.1 %copy-start.15 = (f32[512,12]{0,1:T(8,128)S(1)}, f32[512,12]{0,1:T(8,128)}, u32[]{:S(2)}) copy-start(f32[512,12]{0,1:T(8,128)} %copy-done.14) | copy-start | bytes 73732
  136.9 113.2 %all-gather.12.cloned.1.call-start = ((), (), s32[]{:S(2)}) async-start(), calls=%async_computation.2 | async-start | bytes 7077888 | tf_op jit(solution)/shard_map/all_gather | solution.py:151
  162.3 225.3 %all-gather.20.cloned.1.call-start = ((), (), s32[]{:S(2)}) async-start(), calls=%async_computation.6 | async-start | bytes 5308416 | tf_op jit(solution)/shard_map/all_gather | solution.py:182
  162.9 287.4 %all-gather.18.cloned.1.call-start = ((), (), s32[]{:S(2)}) async-start(), calls=%async_computation.5 | async-start | bytes 3932160 | tf_op jit(solution)/shard_map/all_gather | solution.py:177
  270.8 11.7 %copy-start = (f32[512,768]{0,1:T(8,128)S(1)}, f32[512,768]{0,1:T(8,128)}, u32[]{:S(2)}) copy-start(f32[512,768]{0,1:T(8,128)} %get-tuple-element.274) | copy-start | bytes 4718596 | tf_op jit(solution)/shard_map/while
  282.5 0.8 copy-start.7
  283.0 1.2 copy-start.1
  283.2 0.9 copy-start.8
  304.9 10.9 %copy-start = (f32[512,768]{0,1:T(8,128)S(1)}, f32[512,768]{0,1:T(8,128)}, u32[]{:S(2)}) copy-start(f32[512,768]{0,1:T(8,128)} %get-tuple-element.274) | copy-start | bytes 4718596 | tf_op jit(solution)/shard_map/while
  315.8 0.8 copy-start.7
  316.3 1.2 copy-start.1
  316.5 0.9 copy-start.8
  338.2 10.9 %copy-start = (f32[512,768]{0,1:T(8,128)S(1)}, f32[512,768]{0,1:T(8,128)}, u32[]{:S(2)}) copy-start(f32[512,768]{0,1:T(8,128)} %get-tuple-element.274) | copy-start | bytes 4718596 | tf_op jit(solution)/shard_map/while
  349.1 0.8 copy-start.7
  349.6 1.2 copy-start.1
  349.8 0.9 copy-start.8
  371.5 10.9 %copy-start = (f32[512,768]{0,1:T(8,128)S(1)}, f32[512,768]{0,1:T(8,128)}, u32[]{:S(2)}) copy-start(f32[512,768]{0,1:T(8,128)} %get-tuple-element.274) | copy-start | bytes 4718596 | tf_op jit(solution)/shard_map/while
  382.4 0.8 copy-start.7
  382.9 1.2 copy-start.1
  383.1 0.9 copy-start.8
  384.1 66.2 %copy-start.9 = (bf16[512,768]{1,0:T(8,128)(2,1)S(1)}, bf16[512,768]{1,0:T(8,128)(2,1)}, u32[]{:S(2)}) copy-start(bf16[512,768]{1,0:T(8,128)(2,1)} %param.12) | copy-start | bytes 2359300
  384.1 66.2 %copy-start.24 = (pred[512]{0:T(512)(128)(4,1)S(1)}, pred[512]{0:T(512)(128)(4,1)}, u32[]{:S(2)}) copy-start(pred[512]{0:T(512)(128)(4,1)} %subtract_compare_fusion) | copy-start | bytes 1540
Sparse Core Ops, SparseCore 0:
  8.9 66.1 all-gather.7
  77.0 37.5 all-gather.13
  116.5 38.9 all-gather.9
  157.2 45.5 all-gather.15
  204.5 45.5 all-gather.11
  251.8 38.9 all-gather.19
  386.8 63.4 all-gather.17
